TPU v7x, 128 devices: a whole 4x4x4 slice. The times are simulated.
128 devices in a mesh: row: 8 (over z, x_lo), col: 16 (over y, x_hi, core).
Axes of the slice: x: 4 (x_hi: 2, x_lo: 2; x = x_hi * 2 + x_lo), y: 4, z: 4, core: 2. Of those that a mesh axis runs over, the one named last changes fastest.
Arguments:
- tensor_blocks: bfloat16 [8, 384, 6, 128, 128], P('row', 'col'), may hold values from -6 to 6
- block_list: int32 [8, 384, 2], P('row', 'col'), may hold values from 0 to 15, as said below
- occ_green: bfloat16 [2048, 2048], P(('row', 'col')), may hold values from -0.125 to 0.125
- virt_green: bfloat16 [2048, 2048], P(None, ('row', 'col')), may hold values from -0.125 to 0.125
Outputs:
- polarizability: float32 [8, 6, 6], P('row')
Inputs may be any that keep to these rules, and one draw needn't show every extreme that they name: `block_list`: within the 24 blocks of one device the (m, l) pairs are distinct, every atom block occurs as l once or twice and as m once or twice, so at most 2 blocks of one device share an l, and some l is shared by exactly 2.
All inputs are finite; a program needn't handle non-finite values.
Results may differ from a plain program's by a relative error of at most 0.006.
Values may be sent and summed in bfloat16 or wider, within the bound.
No kernel may reach another device: no remote copies, remote signals or barrier semaphores. Data moves between devices by JAX's collectives and lax.ppermute only.
A program may use at most 128 MiB of HBM per device.

v0:
```python
import jax
import jax.numpy as jnp
from jax import lax
from jax.sharding import PartitionSpec as P

CAP = 2


def shards(tensor_blocks, block_list, occ_green, virt_green):
    col_count = lax.axis_size("col")
    blocks = tensor_blocks[0]
    pairs = block_list[0]
    held = blocks.shape[0]
    width = blocks.shape[-1]
    target = pairs[:, 1]
    first_blocks = pairs[:, 0]
    places = jnp.arange(held)
    slot_rank = jnp.sum(
        (target[None, :] == target[:, None]) & (places[None, :] < places[:, None]), axis=1
    )
    select = (target[:, None, None] == jnp.arange(col_count)[None, :, None]) & (
        slot_rank[:, None, None] == jnp.arange(CAP)[None, None, :]
    )
    send_blocks = jnp.einsum(
        "tdk,tpab->dkpab", select.astype(jnp.bfloat16), blocks, preferred_element_type=jnp.float32
    ).astype(jnp.bfloat16)
    send_first = jnp.sum(select.astype(jnp.int32) * (first_blocks + 1)[:, None, None], axis=0) - 1
    recv_blocks, recv_first = (
        lax.all_to_all(send_blocks, "col", split_axis=0, concat_axis=0, tiled=True),
        lax.all_to_all(send_first, "col", split_axis=0, concat_axis=0, tiled=True),
    )
    slot_total = recv_blocks.shape[0] * recv_blocks.shape[1]
    flat_blocks = recv_blocks.reshape(slot_total, recv_blocks.shape[2], width, width)
    placing = (recv_first.reshape(slot_total)[:, None] == jnp.arange(col_count)[None, :]).astype(
        jnp.bfloat16
    )
    dense_parts = jnp.einsum(
        "sm,spab->pmab", placing, flat_blocks, preferred_element_type=jnp.float32
    )
    dense_tensor = dense_parts.astype(jnp.bfloat16).reshape(
        flat_blocks.shape[1], col_count * width, width
    )
    basis_total = dense_tensor.shape[1]
    occ_half = jnp.einsum(
        "nm,pml->pnl",
        lax.all_gather(occ_green, ("row", "col"), axis=0, tiled=True),
        dense_tensor,
        preferred_element_type=jnp.float32,
    ).astype(jnp.bfloat16)
    turned = lax.all_to_all(occ_half, "col", split_axis=1, concat_axis=2, tiled=True)
    both_sides = jnp.einsum(
        "pnl,ls->pns",
        turned,
        lax.all_gather(virt_green, ("row", "col"), axis=1, tiled=True),
        preferred_element_type=jnp.float32,
    ).astype(jnp.bfloat16)
    partial_polar = jnp.einsum(
        "pns,qsn->pq", both_sides, dense_tensor, preferred_element_type=jnp.float32
    )
    polar_total = lax.psum(partial_polar, "col")
    return (polar_total / float(basis_total))[None]


def solution(mesh):
    in_specs = (
        P("row", "col", None, None, None),
        P("row", "col", None),
        P(("row", "col"), None),
        P(None, ("row", "col")),
    )
    out_specs = P("row", None, None)
    return jax.shard_map(shards, mesh=mesh, in_specs=in_specs, out_specs=out_specs, check_vma=False)
```

profile of v0, /device:TPU:0, one launch (start us, length us, event | category | flops | bytes accessed | tf_op | source)
XLA Modules:
  0.0 585.8 jit_solution(11802510145233425043)
XLA Ops:
  6.5 0.0 all-gather.3.cloned.1.call-start
  6.5 0.7 all-gather.3.cloned.1.call-update
  7.3 0.0 all-gather.5.cloned.1.call-start
  7.3 0.7 all-gather.5.cloned.1.call-update
  8.0 0.8 add_bitcast_fusion.1
  8.8 0.2 convert_reduce_fusion
  9.0 0.1 fusion.28
  9.1 0.7 copy.44
  9.8 7.1 %all-to-all-start.1 = ((s32[16,1,2]{2,1,0:T(1,128)}), s32[16,1,2]{2,1,0:T(1,128)S(1)}, u32[]{:S(2)}, u32[]{:S(2)}) async-start(s32[16,1,2]{2,1,0:T(1,128)} %copy.44), calls=%async_computation.1 | async-start | bytes 16384 | tf_op jit(solution)/shard_map/all_to_all | solution.py:30
  16.9 6.1 %fusion.11 = bf16[16,2,6,128,128]{4,0,3,2,1:T(8,128)(2,1)S(1)} fusion(bf16[24,6,128,128]{3,2,1,0:T(8,128)(2,1)} %bitcast.54, pred[24,2]{0,1:T(4,128)(4,1)S(1)} %iota_compare_fusion.3, pred[24,16]{0,1:T(8,128)(4,1)S(1)} %iota_compare_fusion.2), kind=kOutput, calls=%fused_computation.11 | convolution fusion | flops 154141440 | bytes 11010480 | tf_op jit(solution)/shard_map/tdk,tpab->dkpab/dot_general | solution.py:24
  23.0 4.3 copy.43
  27.4 0.0 all-to-all-done.1
  27.4 7.3 %all-to-all-start = ((bf16[16,2,6,128,128]{4,3,2,1,0:T(8,128)(2,1)}), bf16[16,2,6,128,128]{4,3,2,1,0:T(8,128)(2,1)}, u32[]{:S(2)}, u32[]{:S(2)}) async-start(bf16[16,2,6,128,128]{4,3,2,1,0:T(8,128)(2,1)} %copy.43), calls=%async_computation | async-start | bytes 12582912 | tf_op jit(solution)/shard_map/all_to_all | solution.py:29
  34.6 0.5 broadcast.65
  35.2 0.7 reduce.3
  35.8 0.1 eq.73
  35.9 78.0 %all-to-all-done = bf16[16,2,6,128,128]{4,3,2,1,0:T(8,128)(2,1)} async-done(((bf16[16,2,6,128,128]{4,3,2,1,0:T(8,128)(2,1)}), bf16[16,2,6,128,128]{4,3,2,1,0:T(8,128)(2,1)}, u32[]{:S(2)}, u32[]{:S(2)}) %all-to-all-start) | async-done | bytes 6291488 | tf_op jit(solution)/shard_map/all_to_all | solution.py:29
  113.9 6.6 %convert_bitcast_fusion = bf16[6,16,128,128]{3,1,2,0:T(8,128)(2,1)S(1)} fusion(bf16[32,6,128,128]{3,2,1,0:T(8,128)(2,1)} %bitcast.6, s32[32]{0:T(128)S(1)} %eq.73), kind=kOutput, calls=%fused_computation.14 | convolution fusion | flops 102236672 | bytes 9437312 | tf_op jit(solution)/shard_map/sm,spab->pmab/dot_general | solution.py:37
  120.5 0.8 copy.46
  121.3 159.5 %all-gather.3.cloned.1.call-done = bf16[2048,2048]{1,0:T(8,128)(2,1)} async-done(((bf16[16,2048]{1,0:T(8,128)(2,1)}), bf16[2048,2048]{1,0:T(8,128)(2,1)}) %all-gather.3.cloned.1.call-update) | async-done | bytes 8388624 | tf_op jit(solution)/shard_map/all_gather | solution.py:46
  280.8 10.3 %fusion.20 = bf16[6,2048,128]{1,2,0:T(8,128)(2,1)} fusion(bf16[6,2048,128]{2,1,0:T(8,128)(2,1)S(1)} %bitcast.52, bf16[2048,2048]{1,0:T(8,128)(2,1)} %all-gather.3.cloned.1.call-done), kind=kOutput, calls=%fused_computation.15 | convolution fusion | flops 6444023808 | bytes 14680064 | tf_op jit(solution)/shard_map/nm,pml->pnl/dot_general | solution.py:44
  291.2 6.4 %copy.48 = bf16[6,2048,128]{2,0,1:T(8,128)(2,1)} copy(bf16[6,2048,128]{1,2,0:T(8,128)(2,1)} %fusion.20) | data formatting | bytes 6291456 | tf_op jit(solution)/shard_map/convert_element_type | solution.py:49
  297.6 5.4 all-to-all-start.2
  303.0 5.1 copy.53
  308.0 51.2 %all-to-all-done.2 = bf16[6,2048,128]{2,0,1:T(8,128)(2,1)} async-done(((bf16[6,2048,128]{2,0,1:T(8,128)(2,1)}), bf16[6,2048,128]{2,0,1:T(8,128)(2,1)}, u32[]{:S(2)}, u32[]{:S(2)}) %all-to-all-start.2) | async-done | bytes 3145760 | tf_op jit(solution)/shard_map/all_to_all | solution.py:50
  359.3 5.4 copy.50
  364.7 164.0 %all-gather.5.cloned.1.call-done = bf16[2048,2048]{0,1:T(8,128)(2,1)} async-done(((bf16[2048,16]{0,1:T(8,128)(2,1)}), bf16[2048,2048]{0,1:T(8,128)(2,1)}) %all-gather.5.cloned.1.call-update) | async-done | bytes 8388624 | tf_op jit(solution)/shard_map/all_gather | solution.py:54
  528.7 0.0 copy-start
  528.7 9.3 %fusion.17 = bf16[6,128,2048]{2,1,0:T(8,128)(2,1)S(1)} fusion(bf16[6,128,2048]{1,2,0:T(8,128)(2,1)S(1)} %bitcast.55, bf16[2048,2048]{0,1:T(8,128)(2,1)} %all-gather.5.cloned.1.call-done), kind=kOutput, calls=%fused_computation.13 | convolution fusion | flops 6444023808 | bytes 14680064 | tf_op jit(solution)/shard_map/pnl,ls->pns/dot_general | solution.py:51
  538.0 0.0 copy-done
  538.0 5.7 fusion.25
  543.7 34.6 %psum.7 = f32[6,6]{1,0:T(8,128)S(1)} all-reduce(f32[6,6]{1,0:T(8,128)S(1)} %fusion.25), channel_id=1, replica_groups=mesh['row'=8,'col'=16] {'col'}, use_global_device_ids=true, to_apply=%region_2.0 | all-reduce | flops 36 | bytes 288 | tf_op jit(solution)/shard_map/psum | solution.py:60
  578.4 0.6 copy.54
  (4 shorter events, 0.0 us)
Async XLA Ops:
  6.5 274.3 %all-gather.3.cloned.1.call-start = ((), (), s32[]{:S(2)}) async-start(), calls=%async_computation.3 | async-start | bytes 8454144 | tf_op jit(solution)/shard_map/all_gather | solution.py:46
  7.3 521.5 %all-gather.5.cloned.1.call-start = ((), (), s32[]{:S(2)}) async-start(), calls=%async_computation.4 | async-start | bytes 8454144 | tf_op jit(solution)/shard_map/all_gather | solution.py:54
  9.8 17.6 %all-to-all-start.1 = ((s32[16,1,2]{2,1,0:T(1,128)}), s32[16,1,2]{2,1,0:T(1,128)S(1)}, u32[]{:S(2)}, u32[]{:S(2)}) async-start(s32[16,1,2]{2,1,0:T(1,128)} %copy.44), calls=%async_computation.1 | async-start | bytes 16384 | tf_op jit(solution)/shard_map/all_to_all | solution.py:30
  27.4 86.5 %all-to-all-start = ((bf16[16,2,6,128,128]{4,3,2,1,0:T(8,128)(2,1)}), bf16[16,2,6,128,128]{4,3,2,1,0:T(8,128)(2,1)}, u32[]{:S(2)}, u32[]{:S(2)}) async-start(bf16[16,2,6,128,128]{4,3,2,1,0:T(8,128)(2,1)} %copy.43), calls=%async_computation | async-start | bytes 12582912 | tf_op jit(solution)/shard_map/all_to_all | solution.py:29
  297.6 61.7 %all-to-all-start.2 = ((bf16[6,2048,128]{2,0,1:T(8,128)(2,1)}), bf16[6,2048,128]{2,0,1:T(8,128)(2,1)}, u32[]{:S(2)}, u32[]{:S(2)}) async-start(bf16[6,2048,128]{2,0,1:T(8,128)(2,1)} %copy.48), calls=%async_computation.2 | async-start | bytes 8388608 | tf_op jit(solution)/shard_map/all_to_all | solution.py:50
  528.7 9.3 %copy-start = (bf16[6,2048,128]{1,0,2:T(8,128)(2,1)S(1)}, bf16[6,2048,128]{1,0,2:T(8,128)(2,1)}, u32[]{:S(2)}) copy-start(bf16[6,2048,128]{1,0,2:T(8,128)(2,1)} %copy.53) | copy-start | bytes 9437188
Sparse Core Ops, SparseCore 0:
  9.1 271.7 all-gather.2
  282.6 246.1 all-gather.4
where the time goes:
time: 586 us
  waiting for transfers between devices  454 us (77%)
  matrix products  38 us (6%)
  blocking collectives  34.6 us (6%)
  local copies, waits for them, and re-layouts  23.9 us (4%)
  starting transfers between devices  19.8 us (3%)
  between operations  13.5 us (2%)
    all_gather x1, waiting for transfers between devices, shards(): lax.all_gather(virt_green, ('row', 'col'), axis=1, tiled=True)  164 us
    all_gather x1, waiting for transfers between devices, shards(): lax.all_gather(occ_green, ('row', 'col'), axis=0, tiled=True)  160 us
    all_to_all x1, waiting for transfers between devices, shards(): lax.all_to_all(send_blocks, 'col', split_axis=0, concat_axis=0, tiled=True)  78 us
    all_to_all x1, waiting for transfers between devices, shards(): lax.all_to_all(occ_half, 'col', split_axis=1, concat_axis=2, tiled=True)  51.2 us
    psum x1, blocking collectives, shards(): polar_total = lax.psum(partial_polar, 'col')  34.6 us
  transfers between devices with their start and end apart: 5, of which 4 were waited for; matrix products, arithmetic and copies ran while one was open for 8% of the time, Pallas kernels for 0%

commit v1 on v0

--- a/solution.py
+++ b/solution.py
@@ -51,7 +51,12 @@
     both_sides = jnp.einsum(
         "pnl,ls->pns",
         turned,
-        lax.all_gather(virt_green, ("row", "col"), axis=1, tiled=True),
+        jnp.concatenate(
+            lax.all_to_all(
+                jnp.stack([virt_green] * lax.axis_size(("row", "col"))), ("row", "col"), 0, 0
+            ),
+            axis=1,
+        ),
         preferred_element_type=jnp.float32,
     ).astype(jnp.bfloat16)
     partial_polar = jnp.einsum(

time: 586 us -> 522 us (0.89)
  waiting for transfers between devices: 454 us -> 328 us
  blocking collectives: 34.6 us -> 90.6 us
    all_gather x1 -> x0, waiting for transfers between devices: 164 us -> none  [shards(): lax.all_gather(virt_green, ('row', 'col'), axis=1, tiled=True)]
    all_to_all x0 -> x1, blocking collectives: none -> 56.9 us  [shards(): lax.all_to_all(occ_half, 'col', split_axis=1, concat_axis=2, tiled=True)]
    all_to_all x1, waiting for transfers between devices: 51.2 us -> 89.9 us  [shards(): lax.all_to_all(jnp.stack([virt_green] * lax.axis_size(('row', 'col'))), (...]
  transfers between devices with their start and end apart: 5 -> 4, of which waited for: 4 -> 3; matrix products, arithmetic and copies ran while one was open for 8% -> 6% of each run, Pallas kernels for 0% -> 0%
where the time goes in v1:
time: 522 us; the launch traced here: 521 us
  waiting for transfers between devices  328 us (63%)
  blocking collectives  90.6 us (17%)
  matrix products  38 us (7%)
  local copies, waits for them, and re-layouts  28.1 us (5%)
  starting transfers between devices  20.5 us (4%)
  between operations  13.5 us (3%)
    all_gather x1, waiting for transfers between devices, shards(): lax.all_gather(occ_green, ('row', 'col'), axis=0, tiled=True)  160 us
    all_to_all x1, waiting for transfers between devices, shards(): lax.all_to_all(jnp.stack([virt_green] * lax.axis_size(('row', 'col'))), (...  89.9 us
    all_to_all x1, waiting for transfers between devices, shards(): lax.all_to_all(send_blocks, 'col', split_axis=0, concat_axis=0, tiled=True)  77.7 us
    all_to_all x1, blocking collectives, shards(): lax.all_to_all(occ_half, 'col', split_axis=1, concat_axis=2, tiled=True)  56.9 us
    psum x1, blocking collectives, shards(): polar_total = lax.psum(partial_polar, 'col')  33.7 us
  transfers between devices with their start and end apart: 4, of which 3 were waited for; matrix products, arithmetic and copies ran while one was open for 6% of the time, Pallas kernels for 0%

profile of v1, /device:TPU:0, one launch (start us, length us, event | category | flops | bytes accessed | tf_op | source)
XLA Modules:
  0.0 520.9 jit_solution(3034065534698460837)
XLA Ops:
  6.5 0.0 all-gather.2.cloned.1.call-start
  6.5 0.7 all-gather.2.cloned.1.call-update
  7.3 0.8 add_bitcast_fusion.1
  8.0 0.2 convert_reduce_fusion
  8.2 0.1 fusion.23
  8.3 0.7 copy.47
  9.0 7.1 %all-to-all-start.1 = ((s32[16,1,2]{2,1,0:T(1,128)}), s32[16,1,2]{2,1,0:T(1,128)S(1)}, u32[]{:S(2)}, u32[]{:S(2)}) async-start(s32[16,1,2]{2,1,0:T(1,128)} %copy.47), calls=%async_computation.1 | async-start | bytes 16384 | tf_op jit(solution)/shard_map/all_to_all | solution.py:30
  16.2 6.1 %fusion.9 = bf16[16,2,6,128,128]{4,0,3,2,1:T(8,128)(2,1)S(1)} fusion(bf16[24,6,128,128]{3,2,1,0:T(8,128)(2,1)} %bitcast.56, pred[24,2]{0,1:T(4,128)(4,1)S(1)} %iota_compare_fusion.3, pred[24,16]{0,1:T(8,128)(4,1)S(1)} %iota_compare_fusion.2), kind=kOutput, calls=%fused_computation.9 | convolution fusion | flops 154141440 | bytes 11010480 | tf_op jit(solution)/shard_map/tdk,tpab->dkpab/dot_general | solution.py:24
  22.3 4.4 copy.46
  26.7 0.0 all-to-all-done.1
  26.7 7.3 %all-to-all-start = ((bf16[16,2,6,128,128]{4,3,2,1,0:T(8,128)(2,1)}), bf16[16,2,6,128,128]{4,3,2,1,0:T(8,128)(2,1)}, u32[]{:S(2)}, u32[]{:S(2)}) async-start(bf16[16,2,6,128,128]{4,3,2,1,0:T(8,128)(2,1)} %copy.46), calls=%async_computation | async-start | bytes 12582912 | tf_op jit(solution)/shard_map/all_to_all | solution.py:29
  34.0 0.5 broadcast.67
  34.5 0.7 reduce.3
  35.1 0.1 eq.73
  35.2 77.7 %all-to-all-done = bf16[16,2,6,128,128]{4,3,2,1,0:T(8,128)(2,1)} async-done(((bf16[16,2,6,128,128]{4,3,2,1,0:T(8,128)(2,1)}), bf16[16,2,6,128,128]{4,3,2,1,0:T(8,128)(2,1)}, u32[]{:S(2)}, u32[]{:S(2)}) %all-to-all-start) | async-done | bytes 6291488 | tf_op jit(solution)/shard_map/all_to_all | solution.py:29
  112.9 6.6 %convert_bitcast_fusion = bf16[6,16,128,128]{3,1,2,0:T(8,128)(2,1)S(1)} fusion(bf16[32,6,128,128]{3,2,1,0:T(8,128)(2,1)} %bitcast.6, s32[32]{0:T(128)S(1)} %eq.73), kind=kOutput, calls=%fused_computation.12 | convolution fusion | flops 102236672 | bytes 9437312 | tf_op jit(solution)/shard_map/sm,spab->pmab/dot_general | solution.py:37
  119.5 0.8 copy.49
  120.3 160.0 %all-gather.2.cloned.1.call-done = bf16[2048,2048]{1,0:T(8,128)(2,1)} async-done(((bf16[16,2048]{1,0:T(8,128)(2,1)}), bf16[2048,2048]{1,0:T(8,128)(2,1)}) %all-gather.2.cloned.1.call-update) | async-done | bytes 8388624 | tf_op jit(solution)/shard_map/all_gather | solution.py:46
  280.4 10.3 %fusion.15 = bf16[6,2048,128]{1,2,0:T(8,128)(2,1)} fusion(bf16[6,2048,128]{2,1,0:T(8,128)(2,1)S(1)} %bitcast.54, bf16[2048,2048]{1,0:T(8,128)(2,1)} %all-gather.2.cloned.1.call-done), kind=kOutput, calls=%fused_computation.13 | convolution fusion | flops 6444023808 | bytes 14680064 | tf_op jit(solution)/shard_map/nm,pml->pnl/dot_general | solution.py:44
  290.7 6.3 %copy.51 = bf16[6,2048,128]{2,0,1:T(8,128)(2,1)} copy(bf16[6,2048,128]{1,2,0:T(8,128)(2,1)} %fusion.15) | data formatting | bytes 6291456 | tf_op jit(solution)/shard_map/convert_element_type | solution.py:49
  297.0 0.0 copy-start.1
  297.0 56.9 %all_to_all.34 = bf16[6,2048,128]{2,0,1:T(8,128)(2,1)} all-to-all(bf16[6,2048,128]{2,0,1:T(8,128)(2,1)} %copy.51), channel_id=1, replica_groups=mesh['row'=8,'col'=16] {'col'}, dimensions={1} | all-to-all | bytes 6291456 | tf_op jit(solution)/shard_map/all_to_all | solution.py:50
  353.9 0.0 copy-done.1
  353.9 4.3 stack.2
  358.2 6.1 %all-to-all-start.3 = ((bf16[128,2048,16]{1,2,0:T(8,128)(2,1)}), bf16[128,2048,16]{1,2,0:T(8,128)(2,1)}, u32[]{:S(2)}, u32[]{:S(2)}) async-start(bf16[128,2048,16]{1,2,0:T(8,128)(2,1)} %stack.2), calls=%async_computation.3 | async-start | bytes 16777216 | tf_op jit(solution)/shard_map/all_to_all | solution.py:55
  364.3 5.0 copy.57
  369.3 5.4 %copy.53 = bf16[6,128,16,128]{1,3,2,0:T(8,128)(2,1)S(1)} copy(bf16[6,128,16,128]{3,0,1,2:T(8,128)(2,1)} %bitcast.53) | data formatting | bytes 6291456 | tf_op jit(solution)/shard_map/all_to_all | solution.py:50
  374.8 89.9 %all-to-all-done.3 = bf16[128,2048,16]{1,2,0:T(8,128)(2,1)} async-done(((bf16[128,2048,16]{1,2,0:T(8,128)(2,1)}), bf16[128,2048,16]{1,2,0:T(8,128)(2,1)}, u32[]{:S(2)}, u32[]{:S(2)}) %all-to-all-start.3) | async-done | bytes 8388640 | tf_op jit(solution)/shard_map/all_to_all | solution.py:55
  464.7 0.0 copy-start
  464.7 9.3 %convolution_convert_fusion = bf16[6,128,2048]{2,1,0:T(8,128)(2,1)S(1)} fusion(bf16[6,128,2048]{1,2,0:T(8,128)(2,1)S(1)} %bitcast.57, bf16[2048,2048,1]{0,1,2:T(8,128)(2,1)} %bitcast.21), kind=kOutput, calls=%fused_computation.11 | convolution fusion | flops 6444023808 | bytes 14680064 | tf_op jit(solution)/shard_map/pnl,ls->pns/dot_general | solution.py:51
  474.0 0.0 copy-done
  474.0 5.7 %fusion.20 = f32[6,6]{1,0:T(8,128)S(1)} fusion(bf16[6,2048,128]{1,0,2:T(8,128)(2,1)S(1)} %copy-done, bf16[6,128,2048]{2,1,0:T(8,128)(2,1)S(1)} %convolution_convert_fusion), kind=kOutput, calls=%fused_computation.14 | convolution fusion | flops 18874368 | bytes 6291600 | tf_op jit(solution)/shard_map/pns,qsn->pq/dot_general | solution.py:62
  479.7 33.7 %psum.7 = f32[6,6]{1,0:T(8,128)S(1)} all-reduce(f32[6,6]{1,0:T(8,128)S(1)} %fusion.20), channel_id=1, replica_groups=mesh['row'=8,'col'=16] {'col'}, use_global_device_ids=true, to_apply=%region_2.0 | all-reduce | flops 36 | bytes 288 | tf_op jit(solution)/shard_map/psum | solution.py:65
  513.4 0.6 copy.58
  (4 shorter events, 0.0 us)
Async XLA Ops:
  6.5 273.8 %all-gather.2.cloned.1.call-start = ((), (), s32[]{:S(2)}) async-start(), calls=%async_computation.4 | async-start | bytes 8454144 | tf_op jit(solution)/shard_map/all_gather | solution.py:46
  9.0 17.6 %all-to-all-start.1 = ((s32[16,1,2]{2,1,0:T(1,128)}), s32[16,1,2]{2,1,0:T(1,128)S(1)}, u32[]{:S(2)}, u32[]{:S(2)}) async-start(s32[16,1,2]{2,1,0:T(1,128)} %copy.47), calls=%async_computation.1 | async-start | bytes 16384 | tf_op jit(solution)/shard_map/all_to_all | solution.py:30
  26.7 86.2 %all-to-all-start = ((bf16[16,2,6,128,128]{4,3,2,1,0:T(8,128)(2,1)}), bf16[16,2,6,128,128]{4,3,2,1,0:T(8,128)(2,1)}, u32[]{:S(2)}, u32[]{:S(2)}) async-start(bf16[16,2,6,128,128]{4,3,2,1,0:T(8,128)(2,1)} %copy.46), calls=%async_computation | async-start | bytes 12582912 | tf_op jit(solution)/shard_map/all_to_all | solution.py:29
  297.0 56.9 %copy-start.1 = (bf16[2048,16]{0,1:T(8,128)(2,1)S(1)}, bf16[2048,16]{0,1:T(8,128)(2,1)}, u32[]{:S(2)}) copy-start(bf16[2048,16]{0,1:T(8,128)(2,1)} %param.7) | copy-start | bytes 196612
  358.2 106.5 %all-to-all-start.3 = ((bf16[128,2048,16]{1,2,0:T(8,128)(2,1)}), bf16[128,2048,16]{1,2,0:T(8,128)(2,1)}, u32[]{:S(2)}, u32[]{:S(2)}) async-start(bf16[128,2048,16]{1,2,0:T(8,128)(2,1)} %stack.2), calls=%async_computation.3 | async-start | bytes 16777216 | tf_op jit(solution)/shard_map/all_to_all | solution.py:55
  464.7 9.3 %copy-start = (bf16[6,2048,128]{1,0,2:T(8,128)(2,1)S(1)}, bf16[6,2048,128]{1,0,2:T(8,128)(2,1)}, u32[]{:S(2)}) copy-start(bf16[6,2048,128]{1,0,2:T(8,128)(2,1)} %copy.57) | copy-start | bytes 9437188
Sparse Core Ops, SparseCore 0:
  9.1 271.2 all-gather.1
